TPU v7x, 32 devices: a whole 2x2x4 slice. The times are simulated.
32 devices in a mesh: tile: 4 (over x, core), row: 8 (over z, y).
Axes of the slice: x: 2, y: 2, z: 4, core: 2. Of those that a mesh axis runs over, the one named last changes fastest.
Arguments:
- factor_u: bfloat16 [3072, 96, 512], P(('tile', 'row')), may hold values from -0.625 to 0.625
- factor_v: bfloat16 [3072, 96, 512], P(('tile', 'row')), may hold values from -0.25 to 0.25
- tile_ranks: int32 [3072], P(('tile', 'row')), may hold values from 16 to 96
- tile_rows: int32 [3072, 1], P(('tile', 'row')), may hold values from 0 to 31; in each aligned block of 96 rows (0 to 95, 96 to 191, ...) at most 3 rows name the same one
- tile_cols: int32 [3072], P(('tile', 'row')), may hold values from 0 to 31
- cluster_home: int32 [32], replicated, may hold values from 0 to 31, each once
- quad_weights: float32 [32, 512], replicated, may hold values from 0.3 to 3
- test_matrix: bfloat16 [512, 128], replicated, may hold values from -6 to 6
- near_sketch: bfloat16 [32, 512, 128], P(('tile', 'row')), may hold values from -24 to 24
Outputs:
- couplings: float32 [3072, 128, 128], P(('tile', 'row'))
Inputs may be any that keep to these rules, and one draw needn't show every extreme that they name: `tile_rows`: among the 96 tiles of one device no row cluster appears more than 3 times, and in some devices one appears exactly 3 times. `cluster_home`: each of 0 to 31 appears once; the home index is the device's index along tile+row.
All inputs are finite; a program needn't handle non-finite values.
Results may differ from a plain program's by a relative error of at most 0.0074.
Values may be sent and summed in bfloat16 or wider, within the bound.
A program may use at most 192 MiB of HBM per device.

v0:
```python
import jax
import jax.numpy as jnp
from jax import lax
from jax.sharding import PartitionSpec as P


def per_device(
    factor_u,
    factor_v,
    tile_ranks,
    tile_rows,
    tile_cols,
    cluster_home,
    quad_weights,
    test_matrix,
    near_sketch,
):
    tiles, rank_max, nodes = factor_u.shape
    basis_cols = test_matrix.shape[1]
    clusters = cluster_home.shape[0]
    slot_most = max(2, (tiles + clusters - 1) // clusters)
    live_cols = lax.broadcasted_iota(jnp.int32, (tiles, rank_max), 1) < tile_ranks[:, None]
    masked_u = jnp.where(live_cols[:, :, None], factor_u, jnp.zeros((), jnp.bfloat16))
    weighted_v = (factor_v.astype(jnp.float32) * quad_weights[tile_cols][:, None, :]).astype(
        jnp.bfloat16
    )
    sketch = jnp.dot(
        weighted_v.reshape(tiles * rank_max, nodes), test_matrix, preferred_element_type=jnp.float32
    )
    sketch = sketch.astype(jnp.bfloat16).reshape(tiles, rank_max, basis_cols)
    home_index = cluster_home[tile_rows[:, 0]]
    hits = (home_index[:, None] == lax.broadcasted_iota(jnp.int32, (tiles, clusters), 1)).astype(
        jnp.int32
    )
    before = jnp.cumsum(hits, axis=0) - hits
    flat_index = home_index * slot_most + jnp.sum(before * hits, axis=1)
    packed = jnp.concatenate([masked_u, sketch], axis=2)
    outbox = (
        jnp.zeros((clusters * slot_most, rank_max, nodes + basis_cols), jnp.bfloat16)
        .at[flat_index]
        .set(packed)
    )
    inbox = lax.all_to_all(outbox, ("tile", "row"), split_axis=0, concat_axis=0, tiled=True)
    recv_u = inbox[:, :, :nodes].reshape(clusters * slot_most * rank_max, nodes)
    recv_w = inbox[:, :, nodes:].reshape(clusters * slot_most * rank_max, basis_cols)
    far_part = lax.dot_general(
        recv_u, recv_w, (((0,), (0,)), ((), ())), preferred_element_type=jnp.float32
    )
    sketched = near_sketch[0].astype(jnp.float32) + far_part
    gram_matrix = jnp.dot(
        sketched.T, sketched, precision=lax.Precision.HIGHEST, preferred_element_type=jnp.float32
    )
    lower_factor = jnp.linalg.cholesky(gram_matrix)
    basis_rows = lax.linalg.triangular_solve(lower_factor, sketched.T, left_side=True, lower=True)
    basis_half = basis_rows.astype(jnp.bfloat16)
    projected = lax.dot_general(
        recv_u, basis_half, (((1,), (1,)), ((), ())), preferred_element_type=jnp.float32
    )
    projected = projected.astype(jnp.bfloat16).reshape(clusters * slot_most, rank_max, basis_cols)
    returned = lax.all_to_all(projected, ("tile", "row"), split_axis=0, concat_axis=0, tiled=True)
    own_proj = returned[flat_index]
    return jnp.einsum("tkc,tke->tce", own_proj, sketch, preferred_element_type=jnp.float32)


def solution(mesh):
    placed = (
        P(("tile", "row"), None, None),
        P(("tile", "row"), None, None),
        P(("tile", "row")),
        P(("tile", "row"), None),
        P(("tile", "row")),
        P(),
        P(),
        P(),
        P(("tile", "row"), None, None),
    )
    return jax.shard_map(
        per_device,
        mesh=mesh,
        in_specs=placed,
        out_specs=P(("tile", "row"), None, None),
        check_vma=False,
    )
```

profile of v0, /device:TPU:0, one launch (start us, length us, event | category | flops | bytes accessed | tf_op | source)
XLA Modules:
  0.0 450.2 jit_solution(1907050796962145389)
XLA Ops:
  0.0 0.0 copy-start
  0.0 0.7 fusion.12
  0.7 1.6 gather_fusion
  2.3 0.1 fusion.11
  2.4 0.1 reduce_window_sum.11
  2.5 0.2 select_reduce_fusion.1
  2.7 0.7 compare_select_fusion
  3.4 0.7 iota_compare_fusion.2
  4.1 1.6 gather_fusion.1
  5.8 11.0 %multiply_convert_fusion = bf16[96,96,512]{2,1,0:T(8,128)(2,1)} fusion(bf16[96,96,512]{2,1,0:T(8,128)(2,1)} %param.10, f32[96,512]{1,0:T(8,128)S(1)} %gather_fusion.1), kind=kLoop, calls=%fused_computation.4 | loop fusion | flops 14155776 | bytes 19070976 | tf_op jit(solution)/shard_map/convert_element_type | solution.py:24
  16.8 6.3 %convolution_convert_fusion.1 = bf16[9216,128]{1,0:T(8,128)(2,1)S(1)} fusion(bf16[9216,512]{1,0:T(8,128)(2,1)} %bitcast.36, bf16[512,128]{1,0:T(8,128)(2,1)S(1)} %copy-done), kind=kOutput, calls=%fused_computation.7 | convolution fusion | flops 1209139200 | bytes 11927552 | tf_op jit(solution)/shard_map/dot_general | solution.py:27
  23.1 5.7 %broadcast_select_fusion = bf16[96,96,512]{2,1,0:T(8,128)(2,1)S(1)} fusion(bf16[96,96,512]{2,1,0:T(8,128)(2,1)} %param.9, pred[96,96]{1,0:T(8,128)(4,1)S(1)} %iota_compare_fusion.2), kind=kLoop, calls=%fused_computation.8 | loop fusion | flops 4718592 | bytes 18883584 | tf_op jit(solution)/shard_map/jit(_where)/select_n | solution.py:23
  28.8 5.2 %pad_maximum_fusion = bf16[96,96,640]{2,1,0:T(8,128)(2,1)} fusion(bf16[96,96,128]{2,1,0:T(8,128)(2,1)S(1)} %bitcast.37, bf16[96,96,512]{2,1,0:T(8,128)(2,1)S(1)} %broadcast_select_fusion), kind=kLoop, calls=%fused_computation.5 | loop fusion | flops 23592960 | bytes 23592960 | tf_op jit(solution)/shard_map/concatenate | solution.py:37
  34.0 5.3 %broadcast_in_dim.18 = bf16[96,96,640]{2,1,0:T(8,128)(2,1)} broadcast(bf16[]{:T(256)} %constant.48.clone.1), dimensions={} | broadcast | bytes 11796482 | tf_op jit(solution)/shard_map/broadcast_in_dim | solution.py:39
  39.3 32.5 %scatter_fusion = bf16[96,96,640]{2,1,0:T(8,128)(2,1)} fusion(bf16[96,96,640]{2,1,0:T(8,128)(2,1)} %broadcast_in_dim.18, s32[96]{0:T(128)S(1)} %fusion.13, bf16[96,96,640]{2,1,0:T(8,128)(2,1)} %pad_maximum_fusion), kind=kCustom, calls=%fused_computation.3 | custom fusion | bytes 35389824 | tf_op jit(solution)/shard_map/scatter | solution.py:41
  71.8 265.1 %all_to_all.10 = bf16[96,96,640]{2,1,0:T(8,128)(2,1)S(1)} all-to-all(bf16[96,96,640]{2,1,0:T(8,128)(2,1)} %scatter_fusion), channel_id=1, replica_groups=mesh['tile'=4,'row'=8] {'tile','row'}, dimensions={0} | all-to-all | bytes 23592960 | tf_op jit(solution)/shard_map/all_to_all | solution.py:43
  336.9 2.7 fusion.5
  339.7 1.7 copy-done.2
  341.3 0.6 fusion.15
  341.9 0.1 copy.11
  342.0 11.7 %cholesky.16 = f32[128,128]{1,0:T(8,128)S(1)} custom-call(f32[128,128]{1,0:T(8,128)S(1)} %fusion.10), custom_call_target="Cholesky" | custom-call | tf_op jit(solution)/shard_map/jit(cholesky)/cholesky | solution.py:53
  353.8 0.6 compare_reduce_fusion
  354.4 0.7 fusion.8
  355.1 9.8 %custom-call.6 = f32[1,128,128]{1,2,0:T(8,128)S(1)} custom-call(f32[1,128,128]{2,1,0:T(8,128)S(1)} %fusion.8), custom_call_target="InvertDiagBlocksLowerTriangular" | custom-call | tf_op jit(solution)/shard_map/triangular_solve | solution.py:54
  364.9 0.4 convolution_convert_fusion.2
  365.3 8.4 %slice.24 = bf16[96,96,512]{2,1,0:T(8,128)(2,1)} slice(bf16[96,96,640]{2,1,0:T(8,128)(2,1)} %copy-done.2), slice={[0:96], [0:96], [0:512]} | slice | bytes 18874368 | tf_op jit(solution)/shard_map/slice | solution.py:44
  373.7 7.7 %convolution_convert_fusion = bf16[9216,128]{1,0:T(8,128)(2,1)} fusion(bf16[9216,512]{1,0:T(8,128)(2,1)} %bitcast.35, bf16[128,512]{1,0:T(8,128)(2,1)S(1)} %convolution_convert_fusion.2), kind=kOutput, calls=%fused_computation.6 | convolution fusion | flops 1209139200 | bytes 11927552 | tf_op jit(solution)/shard_map/dot_general | solution.py:56
  381.4 3.6 all-to-all-start.1
  385.1 55.7 %all-to-all-done.1 = bf16[96,96,128]{2,1,0:T(8,128)(2,1)} async-done(((bf16[96,96,128]{2,1,0:T(8,128)(2,1)}), bf16[96,96,128]{2,1,0:T(8,128)(2,1)}, u32[]{:S(2)}, u32[]{:S(2)}) %all-to-all-start.1) | async-done | bytes 2359328 | tf_op jit(solution)/shard_map/all_to_all | solution.py:60
  440.8 4.0 gather_fusion.2
  444.8 5.4 %fusion.16 = f32[96,128,128]{2,1,0:T(8,128)} fusion(bf16[96,96,128]{2,1,0:T(8,128)(2,1)} %gather_fusion.2, bf16[96,96,128]{2,1,0:T(8,128)(2,1)S(1)} %bitcast.38), kind=kOutput, calls=%fused_computation.37 | convolution fusion | flops 301989888 | bytes 11010048 | tf_op jit(solution)/shard_map/tkc,tke->tce/dot_general | solution.py:62
  450.2 0.0 copy-done.1
  (11 shorter events, 0.1 us)
Async XLA Ops:
  0.0 16.8 %copy-start = (bf16[512,128]{1,0:T(8,128)(2,1)S(1)}, bf16[512,128]{1,0:T(8,128)(2,1)}, u32[]{:S(2)}) copy-start(bf16[512,128]{1,0:T(8,128)(2,1)} %param.16) | copy-start | bytes 393220
  71.8 265.1 %copy-start.3 = (bf16[1,512,128]{2,1,0:T(8,128)(2,1)S(1)}, bf16[1,512,128]{2,1,0:T(8,128)(2,1)}, u32[]{:S(2)}) copy-start(bf16[1,512,128]{2,1,0:T(8,128)(2,1)} %param.17) | copy-start | bytes 393220
  336.9 4.4 copy-start.2
  381.4 68.8 %copy-start.1 = (bf16[512,128]{1,0:T(8,128)(2,1)S(1)}, bf16[512,128]{1,0:T(8,128)(2,1)}, u32[]{:S(2)}) copy-start(bf16[512,128]{1,0:T(8,128)(2,1)} %param.16) | copy-start | bytes 393220
  381.4 59.4 %all-to-all-start.1 = ((bf16[96,96,128]{2,1,0:T(8,128)(2,1)}), bf16[96,96,128]{2,1,0:T(8,128)(2,1)}, u32[]{:S(2)}, u32[]{:S(2)}) async-start(bf16[96,96,128]{2,1,0:T(8,128)(2,1)} %bitcast.39), calls=%async_computation.1 | async-start | bytes 4718592 | tf_op jit(solution)/shard_map/all_to_all | solution.py:60
where the time goes:
time: 451 us; the launch traced here: 450 us
  blocking collectives  265 us (59%)
  waiting for transfers between devices  55.7 us (12%)
  local copies, waits for them, and re-layouts  55.2 us (12%)
  other arithmetic  47.3 us (10%)
  matrix products  23.2 us (5%)
    all_to_all x1, blocking collectives, per_device(): lax.all_to_all(outbox, ('tile', 'row'), split_axis=0, concat_axis=0, tile...  265 us
    all_to_all x1, waiting for transfers between devices, per_device(): lax.all_to_all(projected, ('tile', 'row'), split_axis=0, concat_axis=0, t...  55.7 us
    scatter x1, local copies, waits for them, and re-layouts, per_device(): outbox = jnp.zeros((clusters * slot_most, rank_max, nodes + basis_cols),...  32.5 us
    another operation x3, other arithmetic, per_device(): lower_factor = jnp.linalg.cholesky(gram_matrix)  12.4 us
    convert_element_type x1, other arithmetic, per_device(): (factor_v.astype(jnp.float32) * quad_weights[tile_cols][:, None, :]).asty...  11 us
    another operation x2, other arithmetic, per_device(): lax.linalg.triangular_solve(lower_factor, sketched.T, left_side=True, low...  10.5 us
  transfers between devices with their start and end apart: 1, of which 1 were waited for; matrix products, arithmetic and copies ran while one was open for 0% of the time, Pallas kernels for 0%

commit v1 on v0

v1 whole, which is shorter than its diff:
```python
import functools

import jax
import jax.numpy as jnp
from jax import lax
from jax.experimental import pallas as pl
from jax.experimental.pallas import tpu as pltpu
from jax.sharding import PartitionSpec as P

MESH = pl.DeviceIdType.MESH
DEPTH = 4
VMEM = pl.BlockSpec(memory_space=pltpu.VMEM)


def grid_of(sizes):
    return {"x": sizes[0] // 2, "z": DEPTH, "y": sizes[1] // DEPTH}


def where_am_i(sizes):
    dims = grid_of(sizes)
    tile, row = lax.axis_index("tile"), lax.axis_index("row")
    here = {"x": tile // 2, "z": row // dims["y"], "y": row % dims["y"]}
    return dims, here, tile % 2


def device(dims, here, core, **moved):
    at = dict(here, **moved)
    return (at["x"] * 2 + core, at["z"] * dims["y"] + at["y"])


def greet(dims, here, core):
    barrier = pltpu.get_barrier_semaphore()
    pl.semaphore_signal(barrier, inc=1, device_id=device(dims, here, 1 - core), device_id_type=MESH)
    for axis, extent in dims.items():
        place = here[axis]

        @pl.when(place > 0)
        def _():
            pl.semaphore_signal(barrier, inc=1, device_id=device(dims, here, core, **{axis: place - 1}), device_id_type=MESH)

        @pl.when(place < extent - 1)
        def _():
            pl.semaphore_signal(barrier, inc=1, device_id=device(dims, here, core, **{axis: place + 1}), device_id_type=MESH)

    heard = 1
    for axis, extent in dims.items():
        heard = heard + jnp.where(here[axis] > 0, 1, 0) + jnp.where(here[axis] < extent - 1, 1, 0)
    pl.semaphore_wait(barrier, heard)


PARTS = ((0, 48, ("z", "x", "y")), (48, 48, ("x", "y", "z")), (96, 32, ("y", "z", "x")))
AXES = ("x", "z", "y")


def view(here, done, fixed, start, rows, core=None):
    index = []
    for axis in AXES:
        if axis in fixed:
            index.append(fixed[axis])
        elif axis in done:
            index.append(here[axis])
        else:
            index.append(slice(None))
        if axis == "x" and core is not None:
            index.append(core)
    return tuple(index) + (pl.ds(start, rows), slice(None))


def reduce_kernel(sizes, part_ref, far_ref, held, *scratch):
    boxes, (core_send, core_recv, send_sem, recv_sem) = scratch[:-4], scratch[-4:]
    dims, here, core = where_am_i(sizes)
    greet(dims, here, core)
    sems = {}

    def sem_of(*key):
        return sems.setdefault(key, len(sems))

    box_of = {}
    for number, (_, _, order) in enumerate(PARTS):
        for phase in range(3):
            for way in range(2):
                box_of[number, phase, way] = boxes[len(box_of)]

    core_copies = {}
    for number, (start, rows, _) in enumerate(PARTS):
        copies = []
        for x in range(dims["x"]):
            slot = sem_of("core", number, x)
            copy = pltpu.make_async_remote_copy(
                src_ref=part_ref.at[x, 1 - core, :, :, pl.ds(start, rows), :],
                dst_ref=held.at[x, :, :, pl.ds(start, rows), :],
                send_sem=core_send.at[slot],
                recv_sem=core_recv.at[slot],
                device_id=device(dims, here, 1 - core),
                device_id_type=MESH,
            )
            copy.start()
            copies.append(copy)
        core_copies[number] = copies

    zs, ys = dims["z"], dims["y"]

    def core_sum(number):
        start, rows, _ = PARTS[number]
        for x, copy in enumerate(core_copies[number]):
            copy.wait_recv()

            def add(i, carry):
                z, y = i // ys, i % ys
                own = part_ref[x, core, z, y, pl.ds(start, rows), :].astype(jnp.float32)
                got = held[x, z, y, pl.ds(start, rows), :].astype(jnp.float32)
                held[x, z, y, pl.ds(start, rows), :] = (own + got).astype(jnp.bfloat16)
                return carry

            lax.fori_loop(0, zs * ys, add, 0)

    def rest_of(order, phase):
        left = [axis for axis in AXES if axis not in order[: phase + 1]]
        count = 1
        for axis in left:
            count *= dims[axis]
        return left, count

    def each(order, phase, body):
        left, count = rest_of(order, phase)

        def step(i, carry):
            at, rem = {}, i
            for axis in reversed(left):
                at[axis] = rem % dims[axis]
                rem = rem // dims[axis]
            body(at, tuple(at[axis] for axis in left))
            return carry

        if count == 1:
            step(0, 0)
        else:
            lax.fori_loop(0, count, step, 0)

    def link(number, phase, way, goal):
        start, rows, order = PARTS[number]
        axis = order[phase]
        slot = (number * 3 + phase) * 8 + way * 4 + goal
        to = here[axis] + 1 if way == 0 else here[axis] - 1
        return pltpu.make_async_remote_copy(
            src_ref=held.at[view(here, order[:phase], {axis: goal}, start, rows)],
            dst_ref=box_of[number, phase, way].at[goal],
            send_sem=send_sem.at[slot],
            recv_sem=recv_sem.at[slot],
            device_id=device(dims, here, core, **{axis: to}),
            device_id_type=MESH,
        )

    def runs(way, axis, goal):
        place, extent = here[axis], dims[axis]
        sends = place < goal if way == 0 else place > goal
        relays = place > 0 if way == 0 else place < extent - 1
        return sends, relays

    def goals_of(axis):
        extent = dims[axis]
        for i in range(1, extent):
            yield 0, extent - i
            yield 1, i - 1

    def chain(number, phase):
        start, rows, order = PARTS[number]
        axis = order[phase]
        for way, goal in goals_of(axis):
            sends, relays = runs(way, axis, goal)

            @pl.when(sends)
            def _():
                @pl.when(relays)
                def _():
                    link(number, phase, way, goal).wait_recv()

                    def body(at, rest):
                        index = view(here, order[:phase], dict(at, **{axis: goal}), start, rows)
                        total = held[index].astype(jnp.float32) + box_of[number, phase, way][(goal,) + rest].astype(jnp.float32)
                        held[index] = total.astype(jnp.bfloat16)

                    each(order, phase, body)

                link(number, phase, way, goal).start()

    def finish(number, phase):
        start, rows, order = PARTS[number]
        axis = order[phase]
        place, extent = here[axis], dims[axis]

        def total_up(ways):
            for way in ways:
                link(number, phase, way, place).wait_recv()

            def body(at, rest):
                index = view(here, order[:phase], dict(at, **{axis: place}), start, rows)
                total = held[index].astype(jnp.float32)
                for way in ways:
                    total = total + box_of[number, phase, way][(place,) + rest].astype(jnp.float32)
                if phase == 2:
                    far_ref[pl.ds(start, rows), :] = total
                else:
                    held[index] = total.astype(jnp.bfloat16)

            each(order, phase, body)

        pl.when(place == 0)(lambda: total_up((1,)))
        pl.when(place == extent - 1)(lambda: total_up((0,)))
        if extent > 2:
            pl.when((place > 0) & (place < extent - 1))(lambda: total_up((0, 1)))

    def drain(number, phase):
        axis = PARTS[number][2][phase]
        for way, goal in goals_of(axis):
            pl.when(runs(way, axis, goal)[0])(lambda: link(number, phase, way, goal).wait_send())

    core_sum(1)
    chain(1, 0)
    core_sum(2)
    chain(2, 0)
    core_sum(0)
    chain(0, 0)
    finish(1, 0)
    chain(1, 1)
    finish(2, 0)
    chain(2, 1)
    finish(0, 0)
    chain(0, 1)
    finish(1, 1)
    chain(1, 2)
    finish(0, 1)
    chain(0, 2)
    finish(2, 1)
    chain(2, 2)
    finish(0, 2)
    finish(1, 2)
    finish(2, 2)
    for number in range(3):
        for copy in core_copies[number]:
            copy.wait_send()
        for phase in range(3):
            drain(number, phase)


def spread_kernel(sizes, basis_ref, all_ref, core_send, core_recv, send_sem, recv_sem, own_sem):
    dims, here, core = where_am_i(sizes)
    own = pltpu.make_async_copy(basis_ref, all_ref.at[here["x"], core, here["z"], here["y"]], own_sem)
    own.start()
    greet(dims, here, core)
    own.wait()
    orders = [order[::-1] for _, _, order in PARTS]

    def link(number, phase, way, origin):
        start, rows, _ = PARTS[number]
        order = orders[number]
        axis = order[phase]
        slot = (number * 3 + phase) * 8 + way * 4 + origin
        to = here[axis] + 1 if way == 0 else here[axis] - 1
        rest = [a for a in AXES if a not in order[: phase + 1]]
        block = all_ref.at[view(here, rest, {axis: origin}, start, rows, core)]
        return pltpu.make_async_remote_copy(
            src_ref=block,
            dst_ref=block,
            send_sem=send_sem.at[slot],
            recv_sem=recv_sem.at[slot],
            device_id=device(dims, here, core, **{axis: to}),
            device_id_type=MESH,
        )

    def steps_of(number, phase):
        axis = orders[number][phase]
        place, extent = here[axis], dims[axis]
        for i in range(extent):
            yield i, 0, place - i, place - i >= 0, place < extent - 1
            yield i, 1, place + i, place + i <= extent - 1, place > 0

    def chain(number, phase):
        for i, way, origin, exists, sends in steps_of(number, phase):
            if i == 0:
                pl.when(sends)(lambda: link(number, phase, way, origin).start())
            else:

                @pl.when(exists)
                def _():
                    link(number, phase, way, origin).wait_recv()
                    pl.when(sends)(lambda: link(number, phase, way, origin).start())

    def begin(number, phase):
        for i, way, origin, exists, sends in steps_of(number, phase):
            if i == 0:
                pl.when(sends)(lambda: link(number, phase, way, origin).start())

    def relay(number, phase):
        for i, way, origin, exists, sends in steps_of(number, phase):
            if i > 0:

                @pl.when(exists)
                def _():
                    link(number, phase, way, origin).wait_recv()
                    pl.when(sends)(lambda: link(number, phase, way, origin).start())

    def swap(number):
        start, rows, _ = PARTS[number]
        for x in range(dims["x"]):
            block = all_ref.at[x, core, :, :, pl.ds(start, rows), :]
            yield pltpu.make_async_remote_copy(
                src_ref=block,
                dst_ref=block,
                send_sem=core_send.at[number * dims["x"] + x],
                recv_sem=core_recv.at[number * dims["x"] + x],
                device_id=device(dims, here, 1 - core),
                device_id_type=MESH,
            )

    for phase in range(3):
        for number in range(3):
            if phase == 0:
                begin(number, 0)
        for number in (0, 2, 1) if phase == 0 else (0, 1, 2):
            relay(number, phase)
            if phase < 2:
                begin(number, phase + 1)
            else:
                for copy in swap(number):
                    copy.start()
    for number in range(3):
        for copy in swap(number):
            copy.wait()
        for phase in range(3):
            for i, way, origin, exists, sends in steps_of(number, phase):
                pl.when(exists & sends)(lambda: link(number, phase, way, origin).wait_send())


def sketch_kernel(slots, index_ref, rank_ref, col_ref, *refs):
    u_refs, v_refs = refs[:slots], refs[slots : 2 * slots]
    weights_ref, test_ref, sketch_ref, part_ref = refs[2 * slots :]
    home = pl.program_id(0)
    test = test_ref[...]
    sketches = []
    for slot in range(slots):
        weight = weights_ref[pl.ds(col_ref[home * slots + slot], 1), :]
        weighted = (v_refs[slot][0].astype(jnp.float32) * weight).astype(jnp.bfloat16)
        sketch = jnp.dot(weighted, test, preferred_element_type=jnp.float32)
        live = lax.broadcasted_iota(jnp.int32, sketch.shape, 0) < rank_ref[home * slots + slot]
        sketch = jnp.where(live, sketch, 0.0).astype(jnp.bfloat16)
        sketch_ref[slot] = sketch
        sketches.append(sketch)
    left = jnp.concatenate([u[0] for u in u_refs], axis=0)
    part = lax.dot_general(
        jnp.concatenate(sketches, axis=0), left, (((0,), (0,)), ((), ())), preferred_element_type=jnp.float32
    )
    part_ref[0] = part.astype(jnp.bfloat16)


def couple_kernel(group, home_ref, slot_ref, u_ref, basis_ref, sketch_ref, out_ref):
    first = pl.program_id(0) * group
    for i in range(group):
        basis = basis_ref[home_ref[first + i]]
        projected = lax.dot_general(u_ref[i], basis, (((1,), (1,)), ((), ())), preferred_element_type=jnp.float32)
        out_ref[i] = lax.dot_general(
            projected.astype(jnp.bfloat16), sketch_ref[slot_ref[first + i]], (((0,), (0,)), ((), ())), preferred_element_type=jnp.float32
        )


def per_device(
    sizes,
    factor_u,
    factor_v,
    tile_ranks,
    tile_rows,
    tile_cols,
    cluster_home,
    quad_weights,
    test_matrix,
    near_sketch,
):
    tiles, rank_max, nodes = factor_u.shape
    columns = test_matrix.shape[1]
    clusters = cluster_home.shape[0]
    slots = max(2, (tiles + clusters - 1) // clusters)
    dims = grid_of(sizes)
    homes = jnp.sum(jnp.where(tile_rows == lax.broadcasted_iota(jnp.int32, (tiles, clusters), 1), cluster_home[None, :], 0), axis=1)
    order = lax.broadcasted_iota(jnp.int32, (tiles, tiles), 0)
    earlier = (homes[:, None] == homes[None, :]) & (lax.broadcasted_iota(jnp.int32, (tiles, tiles), 1) < order)
    places = homes * slots + jnp.sum(earlier.astype(jnp.int32), axis=1)
    taken = places[None, :] == lax.broadcasted_iota(jnp.int32, (clusters * slots, tiles), 0)
    pick = lambda values: jnp.sum(jnp.where(taken, values[None, :], 0), axis=1)
    index, ranks, cols = pick(jnp.arange(tiles, dtype=jnp.int32)), pick(tile_ranks), pick(tile_cols)

    def tile_spec(slot):
        return pl.BlockSpec((1, rank_max, nodes), lambda h, index, ranks, cols: (index[h * slots + slot], 0, 0))

    sketch, parts = pl.pallas_call(
        functools.partial(sketch_kernel, slots),
        grid_spec=pltpu.PrefetchScalarGridSpec(
            num_scalar_prefetch=3,
            grid=(clusters,),
            in_specs=[tile_spec(slot) for slot in range(slots)] * 2
            + [
                pl.BlockSpec(quad_weights.shape, lambda h, *_: (0, 0)),
                pl.BlockSpec(test_matrix.shape, lambda h, *_: (0, 0)),
            ],
            out_specs=[
                pl.BlockSpec((slots, rank_max, columns), lambda h, *_: (h, 0, 0)),
                pl.BlockSpec((1, columns, nodes), lambda h, *_: (h, 0, 0)),
            ],
        ),
        out_shape=[
            jax.ShapeDtypeStruct((clusters * slots, rank_max, columns), jnp.bfloat16),
            jax.ShapeDtypeStruct((clusters, columns, nodes), jnp.bfloat16),
        ],
        name="sketch",
    )(index, ranks, cols, *([factor_u] * slots), *([factor_v] * slots), quad_weights, test_matrix)

    shape = (dims["x"], 2, dims["z"], dims["y"], columns, nodes)
    boxes = []
    for _, rows, axes in PARTS:
        for phase in range(3):
            rest = [dims[axis] for axis in AXES if axis not in axes[: phase + 1]]
            boxes += [pltpu.VMEM((dims[axes[phase]], *rest, rows, nodes), jnp.bfloat16)] * 2
    swaps = len(PARTS) * dims["x"]
    sems = [pltpu.SemaphoreType.DMA((swaps,))] * 2 + [pltpu.SemaphoreType.DMA((len(PARTS) * 24,))] * 2
    far_part = pl.pallas_call(
        functools.partial(reduce_kernel, sizes),
        out_shape=jax.ShapeDtypeStruct((columns, nodes), jnp.float32),
        in_specs=[VMEM],
        out_specs=VMEM,
        scratch_shapes=[pltpu.VMEM((shape[0], *shape[2:]), jnp.bfloat16), *boxes, *sems],
        compiler_params=pltpu.CompilerParams(collective_id=0, has_side_effects=True, vmem_limit_bytes=62 << 20),
        name="reduce",
    )(parts.reshape(shape))

    sketched = near_sketch[0].astype(jnp.float32).T + far_part
    gram = lax.dot_general(
        sketched, sketched, (((1,), (1,)), ((), ())), precision=lax.Precision.HIGHEST, preferred_element_type=jnp.float32
    )
    lower = jnp.linalg.cholesky(gram)
    basis = lax.linalg.triangular_solve(lower, sketched, left_side=True, lower=True).astype(jnp.bfloat16)

    bases = pl.pallas_call(
        functools.partial(spread_kernel, sizes),
        out_shape=jax.ShapeDtypeStruct(shape, jnp.bfloat16),
        in_specs=[VMEM],
        out_specs=VMEM,
        scratch_shapes=[*sems, pltpu.SemaphoreType.DMA],
        compiler_params=pltpu.CompilerParams(collective_id=1, has_side_effects=True, vmem_limit_bytes=62 << 20),
        name="spread",
    )(basis).reshape(clusters, columns, nodes)

    group = 8
    return pl.pallas_call(
        functools.partial(couple_kernel, group),
        grid_spec=pltpu.PrefetchScalarGridSpec(
            num_scalar_prefetch=2,
            grid=(tiles // group,),
            in_specs=[
                pl.BlockSpec((group, rank_max, nodes), lambda g, *_: (g, 0, 0)),
                pl.BlockSpec(bases.shape, lambda g, *_: (0, 0, 0), pipeline_mode=pl.Buffered(1)),
                pl.BlockSpec(sketch.shape, lambda g, *_: (0, 0, 0), pipeline_mode=pl.Buffered(1)),
            ],
            out_specs=pl.BlockSpec((group, columns, columns), lambda g, *_: (g, 0, 0)),
        ),
        out_shape=jax.ShapeDtypeStruct((tiles, columns, columns), jnp.float32),
        compiler_params=pltpu.CompilerParams(vmem_limit_bytes=62 << 20),
        name="couple",
    )(homes, places, factor_u, bases, sketch)


def solution(mesh):
    placed = (
        P(("tile", "row"), None, None),
        P(("tile", "row"), None, None),
        P(("tile", "row")),
        P(("tile", "row"), None),
        P(("tile", "row")),
        P(),
        P(),
        P(),
        P(("tile", "row"), None, None),
    )
    sizes = (mesh.shape["tile"], mesh.shape["row"])
    return jax.shard_map(
        functools.partial(per_device, sizes),
        mesh=mesh,
        in_specs=placed,
        out_specs=P(("tile", "row"), None, None),
        check_vma=False,
    )
```

time: 451 us -> 175 us (0.39)
  blocking collectives: 265 us -> 0 us
  Pallas kernels: 0 us -> 144 us
  waiting for transfers between devices: 55.7 us -> 0 us
  local copies, waits for them, and re-layouts: 55.2 us -> 1.1 us
  other arithmetic: 47.3 us -> 25.2 us
  matrix products: 23.2 us -> 3.44 us
    all_to_all x1 -> x0, blocking collectives: 265 us -> none  [per_device(): lax.all_to_all(outbox, ('tile', 'row'), split_axis=0, concat_axis=0, tile...]
    pallas_call x0 -> x4, Pallas kernels: none -> 144 us  [the longest x1 51.4 us: per_device(): pl.pallas_call(functools.partial(reduce_kernel, sizes), out_shape=jax.Sha...]
    all_to_all x1 -> x0, waiting for transfers between devices: 55.7 us -> none  [per_device(): lax.all_to_all(projected, ('tile', 'row'), split_axis=0, concat_axis=0, t...]
    scatter x1 -> x0, local copies, waits for them, and re-layouts: 32.5 us -> none  [per_device(): outbox = jnp.zeros((clusters * slot_most, rank_max, nodes + basis_cols),...]
    dot_general x5 -> x1, matrix products: 22.8 us -> 1.41 us  [per_device(): lax.dot_general(sketched, sketched, (((1,), (1,)), ((), ())), precision=l...]
    convert_element_type x2 -> x0, other arithmetic: 11.1 us -> none  [the longest x1 11 us: per_device(): (factor_v.astype(jnp.float32) * quad_weights[tile_cols][:, None, :]).asty...]
    slice x1 -> x0, local copies, waits for them, and re-layouts: 8.39 us -> none  [per_device(): recv_u = inbox[:, :, :nodes].reshape(clusters * slot_most * rank_max, nodes)]
    gather x3 -> x0, local copies, waits for them, and re-layouts: 7.19 us -> none  [the longest x1 3.98 us: per_device(): own_proj = returned[flat_index]]
  transfers between devices with their start and end apart: 1 -> 0, of which waited for: 1 -> 0; matrix products, arithmetic and copies ran while one was open for 0% -> 0% of each run, Pallas kernels for 0% -> 0%
where the time goes in v1:
time: 175 us; the launch traced here: 174 us
  Pallas kernels  144 us (82%)
  other arithmetic  25.2 us (14%)
  matrix products  3.44 us (2%)
    pallas_call x1, Pallas kernels, per_device(): pl.pallas_call(functools.partial(reduce_kernel, sizes), out_shape=jax.Sha...  51.4 us
    pallas_call x1, Pallas kernels, per_device(): pl.pallas_call(functools.partial(spread_kernel, sizes), out_shape=jax.Sha...  35.5 us
    pallas_call x1, Pallas kernels, per_device(): pl.pallas_call(functools.partial(sketch_kernel, slots), grid_spec=pltpu.P...  28.7 us
    pallas_call x1, Pallas kernels, per_device(): pl.pallas_call(functools.partial(couple_kernel, group), grid_spec=pltpu.P...  28.6 us
    another operation x3, other arithmetic, per_device(): lower = jnp.linalg.cholesky(gram)  12.4 us
    another operation x2, other arithmetic, per_device(): lax.linalg.triangular_solve(lower, sketched, left_side=True, lower=True)  10.5 us

profile of v1, /device:TPU:0, one launch (start us, length us, event | category | flops | bytes accessed | tf_op | source)
XLA Modules:
  0.0 174.1 jit_solution(10758106181838472855)
XLA Ops:
  0.0 0.8 select_reduce_fusion.4.home_ref
  0.8 0.0 copy-start.1
  0.8 0.2 convert_reduce_fusion
  1.0 0.0 copy-start
  1.0 1.4 select_reduce_fusion.1
  2.4 1.0 copy.12
  3.4 28.7 %sketch.1 = (bf16[96,96,128]{2,1,0:T(8,128)(2,1)}, bf16[32,128,512]{2,1,0:T(8,128)(2,1)}) custom-call(s32[96]{0:T(128)} %get-tuple-element.11.index_ref, s32[96]{0:T(128)} %get-tuple-element.10.rank_ref, s32[96]{0:T(128)} %get-tuple-element.9.col_ref, bf16[96,96,512]{2,1,0:T(8,128)(2,1)} %u_ref.1, bf16[96,96,512]{2,1,0:T(8,128)(2,1)} %u_ref.1, ...), custom_call_target="tpu_custom_call" | custom-call | tf_op jit(solution)/shard_map/sketch/pallas_call | solution.py:394
  32.0 0.0 copy-done.1
  32.0 0.0 copy-done
  32.0 51.4 %reduce.7 = f32[128,512]{1,0:T(8,128)} custom-call(bf16[2,2,4,2,128,512]{5,4,3,2,1,0:T(8,128)(2,1)} %bitcast.29), custom_call_target="tpu_custom_call" | custom-call | tf_op jit(solution)/shard_map/reduce/pallas_call | solution.py:424
  83.5 1.4 fusion.2
  84.9 0.1 copy.13
  85.0 11.7 %cholesky.16 = f32[128,128]{1,0:T(8,128)S(1)} custom-call(f32[128,128]{1,0:T(8,128)S(1)} %fusion.8), custom_call_target="Cholesky" | custom-call | tf_op jit(solution)/shard_map/jit(cholesky)/cholesky | solution.py:438
  96.8 0.6 compare_reduce_fusion
  97.4 0.7 fusion.6
  98.1 9.8 %custom-call.6 = f32[1,128,128]{1,2,0:T(8,128)S(1)} custom-call(f32[1,128,128]{2,1,0:T(8,128)S(1)} %fusion.6), custom_call_target="InvertDiagBlocksLowerTriangular" | custom-call | tf_op jit(solution)/shard_map/triangular_solve | solution.py:439
  107.9 2.0 %convolution_convert_fusion.basis_ref = bf16[128,512]{1,0:T(8,128)(2,1)} fusion(f32[128,512]{1,0:T(8,128)} %reduce.7, bf16[1,512,128]{1,2,0:T(8,128)(2,1)S(1)} %copy.12, f32[1,128,128]{1,2,0:T(8,128)S(1)} %custom-call.6), kind=kOutput, calls=%fused_computation | convolution fusion | flops 100859904 | bytes 589824 | tf_op jit(solution)/shard_map/triangular_solve | solution.py:439
  109.9 35.5 %spread.1 = bf16[2,2,4,2,128,512]{5,4,3,2,1,0:T(8,128)(2,1)} custom-call(bf16[128,512]{1,0:T(8,128)(2,1)} %convolution_convert_fusion.basis_ref), custom_call_target="tpu_custom_call" | custom-call | tf_op jit(solution)/shard_map/spread/pallas_call | solution.py:441
  145.4 28.6 %couple.1 = f32[96,128,128]{2,1,0:T(8,128)} custom-call(s32[96]{0:T(128)} %copy-done.1, s32[96]{0:T(128)} %copy-done, bf16[96,96,512]{2,1,0:T(8,128)(2,1)} %u_ref.1, bf16[32,128,512]{2,1,0:T(8,128)(2,1)} %bitcast.28, bf16[96,96,128]{2,1,0:T(8,128)(2,1)} %get-tuple-element.8.sketch_ref), custom_call_target="tpu_custom_call" | custom-call | tf_op jit(solution)/shard_map/couple/pallas_call | solution.py:452
  (3 shorter events, 0.1 us)
Async XLA Ops:
  0.8 31.3 %copy-start.1 = (s32[96]{0:T(128)}, s32[96]{0:T(128)S(1)}, u32[]{:S(2)}) copy-start(s32[96]{0:T(128)S(1)} %select_reduce_fusion.4.home_ref) | copy-start | bytes 1156
  1.0 31.1 %copy-start = (s32[96]{0:T(128)}, s32[96]{0:T(128)S(1)}, u32[]{:S(2)}) copy-start(s32[96]{0:T(128)S(1)} %multiply_add_fusion.slot_ref) | copy-start | bytes 1156

commit v2 on v1

--- a/solution.py
+++ b/solution.py
@@ -163,25 +163,30 @@
             yield 0, extent - i
             yield 1, i - 1
 
-    def chain(number, phase):
+    def begin(number, phase):
+        axis = PARTS[number][2][phase]
+        for way, goal in goals_of(axis):
+            sends, relays = runs(way, axis, goal)
+            pl.when(sends & ~relays)(lambda: link(number, phase, way, goal).start())
+
+    def relay(number, phase):
         start, rows, order = PARTS[number]
         axis = order[phase]
+        if dims[axis] == 2:
+            return
         for way, goal in goals_of(axis):
             sends, relays = runs(way, axis, goal)
 
-            @pl.when(sends)
+            @pl.when(sends & relays)
             def _():
-                @pl.when(relays)
-                def _():
-                    link(number, phase, way, goal).wait_recv()
-
-                    def body(at, rest):
-                        index = view(here, order[:phase], dict(at, **{axis: goal}), start, rows)
-                        total = held[index].astype(jnp.float32) + box_of[number, phase, way][(goal,) + rest].astype(jnp.float32)
-                        held[index] = total.astype(jnp.bfloat16)
-
-                    each(order, phase, body)
-
+                link(number, phase, way, goal).wait_recv()
+
+                def body(at, rest):
+                    index = view(here, order[:phase], dict(at, **{axis: goal}), start, rows)
+                    total = held[index].astype(jnp.float32) + box_of[number, phase, way][(goal,) + rest].astype(jnp.float32)
+                    held[index] = total.astype(jnp.bfloat16)
+
+                each(order, phase, body)
                 link(number, phase, way, goal).start()
 
     def finish(number, phase):
@@ -215,27 +220,18 @@
         for way, goal in goals_of(axis):
             pl.when(runs(way, axis, goal)[0])(lambda: link(number, phase, way, goal).wait_send())
 
-    core_sum(1)
-    chain(1, 0)
-    core_sum(2)
-    chain(2, 0)
-    core_sum(0)
-    chain(0, 0)
-    finish(1, 0)
-    chain(1, 1)
-    finish(2, 0)
-    chain(2, 1)
-    finish(0, 0)
-    chain(0, 1)
-    finish(1, 1)
-    chain(1, 2)
-    finish(0, 1)
-    chain(0, 2)
-    finish(2, 1)
-    chain(2, 2)
-    finish(0, 2)
-    finish(1, 2)
-    finish(2, 2)
+    for number in range(3):
+        core_sum(number)
+        begin(number, 0)
+    relay(0, 0)
+    for phase in range(3):
+        for number in (1, 2, 0):
+            if (number, phase) != (0, 0):
+                relay(number, phase)
+        for number in (1, 2, 0):
+            finish(number, phase)
+            if phase < 2:
+                begin(number, phase + 1)
     for number in range(3):
         for copy in core_copies[number]:
             copy.wait_send()
@@ -275,92 +271,88 @@
             yield i, 0, place - i, place - i >= 0, place < extent - 1
             yield i, 1, place + i, place + i <= extent - 1, place > 0
 
-    def chain(number, phase):
+    def begin(number, phase):
         for i, way, origin, exists, sends in steps_of(number, phase):
             if i == 0:
                 pl.when(sends)(lambda: link(number, phase, way, origin).start())
-            else:
+
+    def relay(number, phase):
+        for i, way, origin, exists, sends in steps_of(number, phase):
+            if i > 0:
 
                 @pl.when(exists)
                 def _():
                     link(number, phase, way, origin).wait_recv()
                     pl.when(sends)(lambda: link(number, phase, way, origin).start())
-
-    def begin(number, phase):
-        for i, way, origin, exists, sends in steps_of(number, phase):
-            if i == 0:
-                pl.when(sends)(lambda: link(number, phase, way, origin).start())
-
-    def relay(number, phase):
-        for i, way, origin, exists, sends in steps_of(number, phase):
-            if i > 0:
-
-                @pl.when(exists)
-                def _():
-                    link(number, phase, way, origin).wait_recv()
-                    pl.when(sends)(lambda: link(number, phase, way, origin).start())
-
-    def swap(number):
+                    swap(number, phase, origin).start()
+
+    def swap(number, phase, origin):
         start, rows, _ = PARTS[number]
-        for x in range(dims["x"]):
-            block = all_ref.at[x, core, :, :, pl.ds(start, rows), :]
-            yield pltpu.make_async_remote_copy(
-                src_ref=block,
-                dst_ref=block,
-                send_sem=core_send.at[number * dims["x"] + x],
-                recv_sem=core_recv.at[number * dims["x"] + x],
-                device_id=device(dims, here, 1 - core),
-                device_id_type=MESH,
-            )
-
+        order = orders[number]
+        rest = [a for a in AXES if a not in order[: phase + 1]]
+        block = all_ref.at[view(here, rest, {order[phase]: origin}, start, rows, core)]
+        slot = (number * 3 + phase) * 4 + origin
+        return pltpu.make_async_remote_copy(
+            src_ref=block,
+            dst_ref=block,
+            send_sem=core_send.at[slot],
+            recv_sem=core_recv.at[slot],
+            device_id=device(dims, here, 1 - core),
+            device_id_type=MESH,
+        )
+
+    for number in range(3):
+        begin(number, 0)
+    for number in range(3):
+        swap(number, 0, here[orders[number][0]]).start()
     for phase in range(3):
-        for number in range(3):
-            if phase == 0:
-                begin(number, 0)
         for number in (0, 2, 1) if phase == 0 else (0, 1, 2):
             relay(number, phase)
             if phase < 2:
                 begin(number, phase + 1)
-            else:
-                for copy in swap(number):
-                    copy.start()
     for number in range(3):
-        for copy in swap(number):
-            copy.wait()
+        swap(number, 0, here[orders[number][0]]).wait()
         for phase in range(3):
             for i, way, origin, exists, sends in steps_of(number, phase):
                 pl.when(exists & sends)(lambda: link(number, phase, way, origin).wait_send())
-
-
-def sketch_kernel(slots, index_ref, rank_ref, col_ref, *refs):
-    u_refs, v_refs = refs[:slots], refs[slots : 2 * slots]
-    weights_ref, test_ref, sketch_ref, part_ref = refs[2 * slots :]
-    home = pl.program_id(0)
+                if i > 0:
+                    pl.when(exists)(lambda: swap(number, phase, origin).wait())
+
+
+def sketch_kernel(homes, slots, index_ref, rank_ref, col_ref, *refs):
+    count = homes * slots
+    u_refs, v_refs = refs[:count], refs[count : 2 * count]
+    weights_ref, test_ref, sketch_ref, part_ref = refs[2 * count :]
+    first = pl.program_id(0) * count
     test = test_ref[...]
     sketches = []
-    for slot in range(slots):
-        weight = weights_ref[pl.ds(col_ref[home * slots + slot], 1), :]
+    for slot in range(count):
+        weight = weights_ref[pl.ds(col_ref[first + slot], 1), :]
         weighted = (v_refs[slot][0].astype(jnp.float32) * weight).astype(jnp.bfloat16)
         sketch = jnp.dot(weighted, test, preferred_element_type=jnp.float32)
-        live = lax.broadcasted_iota(jnp.int32, sketch.shape, 0) < rank_ref[home * slots + slot]
+        live = lax.broadcasted_iota(jnp.int32, sketch.shape, 0) < rank_ref[first + slot]
         sketch = jnp.where(live, sketch, 0.0).astype(jnp.bfloat16)
         sketch_ref[slot] = sketch
         sketches.append(sketch)
-    left = jnp.concatenate([u[0] for u in u_refs], axis=0)
-    part = lax.dot_general(
-        jnp.concatenate(sketches, axis=0), left, (((0,), (0,)), ((), ())), preferred_element_type=jnp.float32
-    )
-    part_ref[0] = part.astype(jnp.bfloat16)
+    for home in range(homes):
+        own = slice(home * slots, (home + 1) * slots)
+        part = lax.dot_general(
+            jnp.concatenate(sketches[own], axis=0),
+            jnp.concatenate([u[0] for u in u_refs[own]], axis=0),
+            (((0,), (0,)), ((), ())),
+            preferred_element_type=jnp.float32,
+        )
+        part_ref[home] = part.astype(jnp.bfloat16)
 
 
 def couple_kernel(group, home_ref, slot_ref, u_ref, basis_ref, sketch_ref, out_ref):
     first = pl.program_id(0) * group
+    projected = [
+        lax.dot_general(basis_ref[home_ref[first + i]], u_ref[i], (((1,), (1,)), ((), ())), preferred_element_type=jnp.float32).astype(jnp.bfloat16)
+        for i in range(group)
+    ]
     for i in range(group):
-        basis = basis_ref[home_ref[first + i]]
-        projected = lax.dot_general(u_ref[i], basis, (((1,), (1,)), ((), ())), preferred_element_type=jnp.float32)
-        out_ref[i] = lax.dot_general(
-            projected.astype(jnp.bfloat16), sketch_ref[slot_ref[first + i]], (((0,), (0,)), ((), ())), preferred_element_type=jnp.float32
-        )
+        out_ref[i] = jnp.dot(projected[i], sketch_ref[slot_ref[first + i]], preferred_element_type=jnp.float32)
 
 
 def per_device(
@@ -388,22 +380,25 @@
     pick = lambda values: jnp.sum(jnp.where(taken, values[None, :], 0), axis=1)
     index, ranks, cols = pick(jnp.arange(tiles, dtype=jnp.int32)), pick(tile_ranks), pick(tile_cols)
 
+    batch = 4
+    count = batch * slots
+
     def tile_spec(slot):
-        return pl.BlockSpec((1, rank_max, nodes), lambda h, index, ranks, cols: (index[h * slots + slot], 0, 0))
+        return pl.BlockSpec((1, rank_max, nodes), lambda h, index, ranks, cols: (index[h * count + slot], 0, 0))
 
     sketch, parts = pl.pallas_call(
-        functools.partial(sketch_kernel, slots),
+        functools.partial(sketch_kernel, batch, slots),
         grid_spec=pltpu.PrefetchScalarGridSpec(
             num_scalar_prefetch=3,
-            grid=(clusters,),
-            in_specs=[tile_spec(slot) for slot in range(slots)] * 2
+            grid=(clusters // batch,),
+            in_specs=[tile_spec(slot) for slot in range(count)] * 2
             + [
                 pl.BlockSpec(quad_weights.shape, lambda h, *_: (0, 0)),
                 pl.BlockSpec(test_matrix.shape, lambda h, *_: (0, 0)),
             ],
             out_specs=[
-                pl.BlockSpec((slots, rank_max, columns), lambda h, *_: (h, 0, 0)),
-                pl.BlockSpec((1, columns, nodes), lambda h, *_: (h, 0, 0)),
+                pl.BlockSpec((count, rank_max, columns), lambda h, *_: (h, 0, 0)),
+                pl.BlockSpec((batch, columns, nodes), lambda h, *_: (h, 0, 0)),
             ],
         ),
         out_shape=[
@@ -411,7 +406,7 @@
             jax.ShapeDtypeStruct((clusters, columns, nodes), jnp.bfloat16),
         ],
         name="sketch",
-    )(index, ranks, cols, *([factor_u] * slots), *([factor_v] * slots), quad_weights, test_matrix)
+    )(index, ranks, cols, *([factor_u] * count), *([factor_v] * count), quad_weights, test_matrix)
 
     shape = (dims["x"], 2, dims["z"], dims["y"], columns, nodes)
     boxes = []
@@ -419,7 +414,7 @@
         for phase in range(3):
             rest = [dims[axis] for axis in AXES if axis not in axes[: phase + 1]]
             boxes += [pltpu.VMEM((dims[axes[phase]], *rest, rows, nodes), jnp.bfloat16)] * 2
-    swaps = len(PARTS) * dims["x"]
+    swaps = len(PARTS) * 12
     sems = [pltpu.SemaphoreType.DMA((swaps,))] * 2 + [pltpu.SemaphoreType.DMA((len(PARTS) * 24,))] * 2
     far_part = pl.pallas_call(
         functools.partial(reduce_kernel, sizes),

time: 175 us -> 144 us (0.82)
  Pallas kernels: 144 us -> 114 us
    pallas_call x1, Pallas kernels: 28.7 us -> 13.8 us  [per_device(): pl.pallas_call(functools.partial(sketch_kernel, batch, slots), grid_spec=...]
    pallas_call x1, Pallas kernels: 28.6 us -> 15.5 us  [per_device(): pl.pallas_call(functools.partial(couple_kernel, group), grid_spec=pltpu.P...]
where the time goes in v2:
time: 144 us
  Pallas kernels  114 us (79%)
  other arithmetic  25.2 us (18%)
  matrix products  3.44 us (2%)
    pallas_call x1, Pallas kernels, per_device(): pl.pallas_call(functools.partial(reduce_kernel, sizes), out_shape=jax.Sha...  50.2 us
    pallas_call x1, Pallas kernels, per_device(): pl.pallas_call(functools.partial(spread_kernel, sizes), out_shape=jax.Sha...  34.2 us
    pallas_call x1, Pallas kernels, per_device(): pl.pallas_call(functools.partial(couple_kernel, group), grid_spec=pltpu.P...  15.5 us
    pallas_call x1, Pallas kernels, per_device(): pl.pallas_call(functools.partial(sketch_kernel, batch, slots), grid_spec=...  13.8 us
    another operation x3, other arithmetic, per_device(): lower = jnp.linalg.cholesky(gram)  12.4 us
    another operation x2, other arithmetic, per_device(): lax.linalg.triangular_solve(lower, sketched, left_side=True, lower=True)  10.5 us

profile of v2, /device:TPU:0, one launch (start us, length us, event | category | flops | bytes accessed | tf_op | source)
XLA Modules:
  0.0 143.6 jit_solution(1963201205034864976)
XLA Ops:
  0.0 0.8 select_reduce_fusion.4.home_ref
  0.8 0.0 copy-start.1
  0.8 0.2 convert_reduce_fusion
  1.0 0.0 copy-start
  1.0 1.4 select_reduce_fusion.1
  2.4 1.0 copy.12
  3.4 13.8 %sketch.1 = (bf16[96,96,128]{2,1,0:T(8,128)(2,1)}, bf16[32,128,512]{2,1,0:T(8,128)(2,1)}) custom-call(s32[96]{0:T(128)} %get-tuple-element.11.index_ref, s32[96]{0:T(128)} %get-tuple-element.10.rank_ref, s32[96]{0:T(128)} %get-tuple-element.9.col_ref, bf16[96,96,512]{2,1,0:T(8,128)(2,1)} %u_ref.1, bf16[96,96,512]{2,1,0:T(8,128)(2,1)} %u_ref.1, ...), custom_call_target="tpu_custom_call" | custom-call | tf_op jit(solution)/shard_map/sketch/pallas_call | solution.py:389
  17.1 0.0 copy-done.1
  17.1 0.0 copy-done
  17.1 50.2 %reduce.7 = f32[128,512]{1,0:T(8,128)} custom-call(bf16[2,2,4,2,128,512]{5,4,3,2,1,0:T(8,128)(2,1)} %bitcast.29), custom_call_target="tpu_custom_call" | custom-call | tf_op jit(solution)/shard_map/reduce/pallas_call | solution.py:419
  67.4 1.4 fusion.2
  68.8 0.1 copy.13
  68.9 11.7 %cholesky.16 = f32[128,128]{1,0:T(8,128)S(1)} custom-call(f32[128,128]{1,0:T(8,128)S(1)} %fusion.8), custom_call_target="Cholesky" | custom-call | tf_op jit(solution)/shard_map/jit(cholesky)/cholesky | solution.py:433
  80.7 0.6 compare_reduce_fusion
  81.3 0.7 fusion.6
  82.0 9.8 %custom-call.6 = f32[1,128,128]{1,2,0:T(8,128)S(1)} custom-call(f32[1,128,128]{2,1,0:T(8,128)S(1)} %fusion.6), custom_call_target="InvertDiagBlocksLowerTriangular" | custom-call | tf_op jit(solution)/shard_map/triangular_solve | solution.py:434
  91.8 2.0 %convolution_convert_fusion.basis_ref = bf16[128,512]{1,0:T(8,128)(2,1)} fusion(f32[128,512]{1,0:T(8,128)} %reduce.7, bf16[1,512,128]{1,2,0:T(8,128)(2,1)S(1)} %copy.12, f32[1,128,128]{1,2,0:T(8,128)S(1)} %custom-call.6), kind=kOutput, calls=%fused_computation | convolution fusion | flops 100859904 | bytes 589824 | tf_op jit(solution)/shard_map/triangular_solve | solution.py:434
  93.8 34.2 %spread.1 = bf16[2,2,4,2,128,512]{5,4,3,2,1,0:T(8,128)(2,1)} custom-call(bf16[128,512]{1,0:T(8,128)(2,1)} %convolution_convert_fusion.basis_ref), custom_call_target="tpu_custom_call" | custom-call | tf_op jit(solution)/shard_map/spread/pallas_call | solution.py:436
  128.0 15.5 %couple.1 = f32[96,128,128]{2,1,0:T(8,128)} custom-call(s32[96]{0:T(128)} %copy-done.1, s32[96]{0:T(128)} %copy-done, bf16[96,96,512]{2,1,0:T(8,128)(2,1)} %u_ref.1, bf16[32,128,512]{2,1,0:T(8,128)(2,1)} %bitcast.28, bf16[96,96,128]{2,1,0:T(8,128)(2,1)} %get-tuple-element.8.sketch_ref), custom_call_target="tpu_custom_call" | custom-call | tf_op jit(solution)/shard_map/couple/pallas_call | solution.py:447
  (3 shorter events, 0.1 us)
Async XLA Ops:
  0.8 16.4 %copy-start.1 = (s32[96]{0:T(128)}, s32[96]{0:T(128)S(1)}, u32[]{:S(2)}) copy-start(s32[96]{0:T(128)S(1)} %select_reduce_fusion.4.home_ref) | copy-start | bytes 1156
  1.0 16.2 %copy-start = (s32[96]{0:T(128)}, s32[96]{0:T(128)S(1)}, u32[]{:S(2)}) copy-start(s32[96]{0:T(128)S(1)} %multiply_add_fusion.slot_ref) | copy-start | bytes 1156

commit v3 on v2

--- a/solution.py
+++ b/solution.py
@@ -345,6 +345,38 @@
         part_ref[home] = part.astype(jnp.bfloat16)
 
 
+BLOCK = 16
+
+
+def basis_kernel(sketched_ref, basis_ref):
+    sketched = sketched_ref[...]
+    size = sketched.shape[0]
+    gram = lax.dot_general(
+        sketched, sketched, (((1,), (1,)), ((), ())), precision=lax.Precision.HIGHEST, preferred_element_type=jnp.float32
+    )
+    eye = lax.broadcasted_iota(jnp.int32, (size, size), 0) == lax.broadcasted_iota(jnp.int32, (size, size), 1)
+    rest = jnp.concatenate([gram, eye.astype(jnp.float32)], axis=1)
+    inverse = []
+    row = lax.broadcasted_iota(jnp.int32, (BLOCK, 1), 0)
+    for start in range(0, size, BLOCK):
+        panel = rest[:BLOCK]
+        for j in range(BLOCK):
+            at = start + j
+            factor = jnp.where(row > j, panel[:, at : at + 1] / panel[j : j + 1, at : at + 1], 0.0)
+            panel = panel - factor * panel[j : j + 1]
+        own = lax.broadcasted_iota(jnp.int32, (BLOCK, size), 1) == row + start
+        pivots = jnp.sum(jnp.where(own, panel[:, :size], 0.0), axis=1, keepdims=True)
+        inverse.append(panel[:, size:] * lax.rsqrt(pivots))
+        if start + BLOCK < size:
+            update = lax.dot_general(
+                panel[:, :size] / pivots, panel, (((0,), (0,)), ((), ())), precision=lax.Precision.HIGHEST, preferred_element_type=jnp.float32
+            )
+            rest = rest[BLOCK:] - update[start + BLOCK :]
+    basis_ref[...] = jnp.dot(
+        jnp.concatenate(inverse, axis=0), sketched, precision=lax.Precision.HIGHEST, preferred_element_type=jnp.float32
+    ).astype(jnp.bfloat16)
+
+
 def couple_kernel(group, home_ref, slot_ref, u_ref, basis_ref, sketch_ref, out_ref):
     first = pl.program_id(0) * group
     projected = [
@@ -427,11 +459,13 @@
     )(parts.reshape(shape))
 
     sketched = near_sketch[0].astype(jnp.float32).T + far_part
-    gram = lax.dot_general(
-        sketched, sketched, (((1,), (1,)), ((), ())), precision=lax.Precision.HIGHEST, preferred_element_type=jnp.float32
-    )
-    lower = jnp.linalg.cholesky(gram)
-    basis = lax.linalg.triangular_solve(lower, sketched, left_side=True, lower=True).astype(jnp.bfloat16)
+    basis = pl.pallas_call(
+        basis_kernel,
+        out_shape=jax.ShapeDtypeStruct((columns, nodes), jnp.bfloat16),
+        in_specs=[VMEM],
+        out_specs=VMEM,
+        name="basis",
+    )(sketched)
 
     bases = pl.pallas_call(
         functools.partial(spread_kernel, sizes),
@@ -443,7 +477,7 @@
         name="spread",
     )(basis).reshape(clusters, columns, nodes)
 
-    group = 8
+    group = 16
     return pl.pallas_call(
         functools.partial(couple_kernel, group),
         grid_spec=pltpu.PrefetchScalarGridSpec(

time: 144 us -> 131 us (0.910)
  other arithmetic: 25.2 us -> 3.99 us
  Pallas kernels: 114 us -> 126 us
  matrix products: 3.44 us -> 0 us
    another operation x5 -> x0, other arithmetic: 22.9 us -> none  [the longest x3 12.4 us: per_device(): lower = jnp.linalg.cholesky(gram)]
    pallas_call x0 -> x1, Pallas kernels: none -> 15.2 us  [per_device(): pl.pallas_call(basis_kernel, out_shape=jax.ShapeDtypeStruct((columns, nod...]
    pallas_call x1, Pallas kernels: 15.5 us -> 12.2 us  [per_device(): pl.pallas_call(functools.partial(couple_kernel, group), grid_spec=pltpu.P...]
    another operation x1 -> x0, matrix products: 2.03 us -> none  [per_device(): lax.linalg.triangular_solve(lower, sketched, left_side=True, lower=True)]
    add x0 -> x1, other arithmetic: none -> 1.68 us  [per_device(): sketched = near_sketch[0].astype(jnp.float32).T + far_part]
where the time goes in v3:
time: 131 us
  Pallas kernels  126 us (96%)
  other arithmetic  3.99 us (3%)
    pallas_call x1, Pallas kernels, per_device(): pl.pallas_call(functools.partial(reduce_kernel, sizes), out_shape=jax.Sha...  50.3 us
    pallas_call x1, Pallas kernels, per_device(): pl.pallas_call(functools.partial(spread_kernel, sizes), out_shape=jax.Sha...  34.2 us
    pallas_call x1, Pallas kernels, per_device(): pl.pallas_call(basis_kernel, out_shape=jax.ShapeDtypeStruct((columns, nod...  15.2 us
    pallas_call x1, Pallas kernels, per_device(): pl.pallas_call(functools.partial(sketch_kernel, batch, slots), grid_spec=...  13.7 us
    pallas_call x1, Pallas kernels, per_device(): pl.pallas_call(functools.partial(couple_kernel, group), grid_spec=pltpu.P...  12.2 us

profile of v3, /device:TPU:0, one launch (start us, length us, event | category | flops | bytes accessed | tf_op | source)
XLA Modules:
  0.0 130.7 jit_solution(12007955278857907721)
XLA Ops:
  0.0 0.8 select_reduce_fusion.3.home_ref
  0.8 0.0 copy-start.1
  0.8 0.2 convert_reduce_fusion
  1.0 0.0 copy-start
  1.0 1.4 %select_reduce_fusion = (s32[96]{0:T(128)}, s32[96]{0:T(128)}, s32[96]{0:T(128)}) fusion(s32[96]{0:T(128)} %param.13, s32[96]{0:T(128)S(1)} %multiply_add_fusion.slot_ref, s32[96]{0:T(128)} %param.11), kind=kLoop, calls=%fused_computation.2 | loop fusion | flops 64224 | bytes 2304 | tf_op jit(solution)/shard_map/reduce_sum | solution.py:412
  2.3 1.0 copy.11
  3.3 13.7 %sketch.1 = (bf16[96,96,128]{2,1,0:T(8,128)(2,1)}, bf16[32,128,512]{2,1,0:T(8,128)(2,1)}) custom-call(s32[96]{0:T(128)} %get-tuple-element.11.index_ref, s32[96]{0:T(128)} %get-tuple-element.10.rank_ref, s32[96]{0:T(128)} %get-tuple-element.9.col_ref, bf16[96,96,512]{2,1,0:T(8,128)(2,1)} %u_ref.1, bf16[96,96,512]{2,1,0:T(8,128)(2,1)} %u_ref.1, ...), custom_call_target="tpu_custom_call" | custom-call | tf_op jit(solution)/shard_map/sketch/pallas_call | solution.py:421
  17.1 0.0 copy-done.1
  17.1 0.0 copy-done
  17.1 50.3 %reduce.1 = f32[128,512]{1,0:T(8,128)} custom-call(bf16[2,2,4,2,128,512]{5,4,3,2,1,0:T(8,128)(2,1)} %bitcast.11), custom_call_target="tpu_custom_call" | custom-call | tf_op jit(solution)/shard_map/reduce/pallas_call | solution.py:451
  67.4 1.7 %fusion.sketched_ref = f32[128,512]{1,0:T(8,128)} fusion(f32[128,512]{1,0:T(8,128)} %reduce.1, bf16[1,512,128]{1,2,0:T(8,128)(2,1)S(1)} %copy.11), kind=kLoop, calls=%fused_computation.1 | loop fusion | flops 131072 | bytes 655360 | tf_op jit(solution)/shard_map/add | solution.py:461
  69.1 15.2 %basis.1.basis_ref = bf16[128,512]{1,0:T(8,128)(2,1)} custom-call(f32[128,512]{1,0:T(8,128)} %fusion.sketched_ref), custom_call_target="tpu_custom_call" | custom-call | tf_op jit(solution)/shard_map/basis/pallas_call | solution.py:462
  84.3 34.2 %spread.1 = bf16[2,2,4,2,128,512]{5,4,3,2,1,0:T(8,128)(2,1)} custom-call(bf16[128,512]{1,0:T(8,128)(2,1)} %basis.1.basis_ref), custom_call_target="tpu_custom_call" | custom-call | tf_op jit(solution)/shard_map/spread/pallas_call | solution.py:470
  118.5 12.2 %couple.1 = f32[96,128,128]{2,1,0:T(8,128)} custom-call(s32[96]{0:T(128)} %copy-done.1, s32[96]{0:T(128)} %copy-done, bf16[96,96,512]{2,1,0:T(8,128)(2,1)} %u_ref.1, bf16[32,128,512]{2,1,0:T(8,128)(2,1)} %bitcast.10, bf16[96,96,128]{2,1,0:T(8,128)(2,1)} %get-tuple-element.8.sketch_ref), custom_call_target="tpu_custom_call" | custom-call | tf_op jit(solution)/shard_map/couple/pallas_call | solution.py:481
  (1 shorter events, 0.0 us)
Async XLA Ops:
  0.8 16.3 %copy-start.1 = (s32[96]{0:T(128)}, s32[96]{0:T(128)S(1)}, u32[]{:S(2)}) copy-start(s32[96]{0:T(128)S(1)} %select_reduce_fusion.3.home_ref) | copy-start | bytes 1156
  1.0 16.2 %copy-start = (s32[96]{0:T(128)}, s32[96]{0:T(128)S(1)}, u32[]{:S(2)}) copy-start(s32[96]{0:T(128)S(1)} %multiply_add_fusion.slot_ref) | copy-start | bytes 1156
